TPU v7x, 32 devices: a whole 2x2x4 slice. The times are simulated.
32 devices in a mesh: groups: 2 (over y), vocab: 8 (over z, x), mp: 2 (over core).
Axes of the slice: x: 2, y: 2, z: 4, core: 2. Of those that a mesh axis runs over, the one named last changes fastest.
Arguments:
- gate_pre: bfloat16 [32, 14336], P(('groups', 'vocab'), 'mp'), parts along dimension 0, may hold values from -6 to 6
- up_pre: bfloat16 [32, 14336], P(('groups', 'vocab'), 'mp'), parts along dimension 0, may hold values from -6 to 6
- down_weight: bfloat16 [8192, 14336], P('vocab', 'mp'), may hold values from -0.046875 to 0.046875
- residual: bfloat16 [32, 8192], P(('groups', 'vocab', 'mp')), parts along dimension 0, may hold values from -36 to 36
- norm_gain: bfloat16 [8192], replicated, may hold values from 0.5 to 1.5
- head_weight: bfloat16 [8192, 4032], P('mp', 'vocab')
- targets: int32 [32], P(('groups', 'mp')), parts along dimension 0, may hold values from 0 to 4031
Outputs:
- log_likelihood: float32 [32], P(('groups', 'mp')), parts along dimension 0
There are 2 independent parts, one for each index of `groups`. A program takes and returns all parts, laid end to end along the dimension named above; an argument that names none is the same for every part. Nothing has to cross between parts.
All inputs are finite; a program needn't handle non-finite values.
Results may differ from a plain program's by a relative error of at most 0.0003.
The roundings to bfloat16 on the way count: a program that leaves them out, or rounds other values in their place, can miss the bound.
Values may be sent and summed in bfloat16 or wider, within the bound.
No kernel may reach another device: no remote copies, remote signals or barrier semaphores. Data moves between devices by JAX's collectives and lax.ppermute only.
A program may use at most 64 MiB of HBM per device.

v0:
```python
import jax
import jax.numpy as jnp
from jax import lax
from jax.sharding import PartitionSpec as P

EPSILON = 1e-05


def merged_2(value, axis, combine):
    everything = jax.tree.map(lambda part: lax.all_gather(part, axis), value)
    first = jax.tree.map(lambda part: part[0], everything)

    def turn(k, so_far):
        return combine(so_far, jax.tree.map(lambda part: part[k], everything))

    return lax.fori_loop(1, lax.axis_size(axis), turn, first)


def merge_stats(earlier, follows):
    joint_max = jnp.maximum(earlier[0], follows[0])
    joint_sum = earlier[1] * jnp.exp(earlier[0] - joint_max) + follows[1] * jnp.exp(
        follows[0] - joint_max
    )
    return (joint_max, joint_sum, earlier[2] + follows[2])


def body(gate_pre, up_pre, down_weight, residual, norm_gain, head_weight, targets):
    vocab_count = lax.axis_size("vocab")
    model_count = lax.axis_size("mp")
    model_index = lax.axis_index("mp")
    vocab_index = lax.axis_index("vocab")
    gated_units = (jax.nn.silu(gate_pre.astype(jnp.float32)) * up_pre.astype(jnp.float32)).astype(
        jnp.bfloat16
    )
    down_terms = lax.dot_general(
        lax.all_gather(gated_units, "vocab", axis=0, tiled=True),
        down_weight,
        (((1,), (1,)), ((), ())),
        preferred_element_type=jnp.float32,
    )
    own_rows = residual.shape[0]
    block_cols = down_weight.shape[0]
    grouped = down_terms.reshape(vocab_count, model_count, own_rows, block_cols)
    arrived = lax.all_to_all(
        lax.all_to_all(grouped, "vocab", split_axis=0, concat_axis=3, tiled=True),
        "mp",
        split_axis=1,
        concat_axis=0,
        tiled=True,
    )
    update = jnp.sum(arrived, axis=(0, 1))
    stream = (residual.astype(jnp.float32) + update).astype(jnp.bfloat16)
    stream = lax.optimization_barrier(stream)
    widened = stream.astype(jnp.float32)
    mean_square = jnp.mean(widened * widened, axis=1, keepdims=True)
    normed = (
        widened * lax.rsqrt(mean_square + EPSILON) * norm_gain.astype(jnp.float32)[None, :]
    ).astype(jnp.bfloat16)
    half_width = head_weight.shape[0]
    halves = lax.dynamic_slice_in_dim(
        lax.all_gather(normed, ("vocab", "mp"), axis=0, tiled=True),
        model_index * half_width,
        half_width,
        1,
    )
    logit_terms = jnp.dot(halves, head_weight, preferred_element_type=jnp.float32)
    logits = lax.psum_scatter(logit_terms, "mp", scatter_dimension=0, tiled=True)
    local_ids = targets - vocab_index * logits.shape[1]
    columns = lax.broadcasted_iota(jnp.int32, logits.shape, 1)
    chosen = jnp.sum(jnp.where(columns == local_ids[:, None], logits, 0.0), axis=1)
    row_top = jnp.max(logits, axis=1)
    exp_total = jnp.sum(jnp.exp(logits - row_top[:, None]), axis=1)
    merged = merged_2((row_top, exp_total, chosen), "vocab", merge_stats)
    return merged[2] - merged[0] - jnp.log(merged[1])


def solution(mesh):
    return jax.shard_map(
        body,
        mesh=mesh,
        in_specs=(
            P(("groups", "vocab"), "mp"),
            P(("groups", "vocab"), "mp"),
            P("vocab", "mp"),
            P(("groups", "vocab", "mp"), None),
            P(),
            P("mp", "vocab"),
            P(("groups", "mp")),
        ),
        out_specs=P(("groups", "mp")),
        check_vma=False,
    )
```

profile of v0, /device:TPU:0, one launch (start us, length us, event | category | flops | bytes accessed | tf_op | source)
XLA Modules:
  0.0 128.8 jit_solution(11626139243467973319)
XLA Ops:
  6.5 0.0 copy-start.3
  6.5 0.0 copy-start.1
  6.5 0.0 copy-start
  6.5 0.0 copy-start.2
  6.5 0.9 fusion.12
  7.4 32.5 %all-gather.3 = bf16[8,2,7168]{2,1,0:T(2,128)(2,1)S(1)} all-gather(bf16[1,2,7168]{2,1,0:T(2,128)(2,1)S(1)} %fusion.12), channel_id=1, replica_groups=mesh['groups'=2,'vocab'=8,'mp'=2] {'vocab'}, dimensions={0}, use_global_device_ids=true | all-gather | bytes 258048 | tf_op jit(solution)/shard_map/all_gather | solution.py:36
  39.9 0.1 reshape.39
  40.0 9.1 %fusion.14 = f32[16,1024]{1,0:T(8,128)S(1)} fusion(bf16[16,7168]{1,0:T(8,128)(2,1)S(1)} %reshape.39, bf16[1024,7168]{1,0:T(8,128)(2,1)} %param.11), kind=kOutput, calls=%fused_computation.28 | convolution fusion | flops 234881024 | bytes 14974976 | tf_op jit(solution)/shard_map/dot_general | solution.py:35
  49.1 0.7 reshape.18
  49.7 5.5 %all-to-all-start = ((f32[8,2,1,1024]{3,1,2,0:T(2,128)}), f32[8,2,1,1024]{3,1,2,0:T(2,128)S(1)}, u32[]{:S(2)}, u32[]{:S(2)}) async-start(f32[8,2,1,1024]{3,1,2,0:T(2,128)} %bitcast.4), calls=%async_computation | async-start | bytes 131072 | tf_op jit(solution)/shard_map/all_to_all | solution.py:45
  55.2 0.0 reduce-scatter.2.cloned.1.call-start
  55.3 0.0 copy-done.1
  55.3 6.8 %all-to-all-done = f32[8,2,1,1024]{3,1,2,0:T(2,128)S(1)} async-done(((f32[8,2,1,1024]{3,1,2,0:T(2,128)}), f32[8,2,1,1024]{3,1,2,0:T(2,128)S(1)}, u32[]{:S(2)}, u32[]{:S(2)}) %all-to-all-start) | async-done | bytes 65568 | tf_op jit(solution)/shard_map/all_to_all | solution.py:45
  62.2 0.1 copy.10
  62.2 3.8 %all_to_all.27 = f32[1,2,1,8192]{3,2,0,1:T(1,128)S(1)} all-to-all(f32[1,2,1,8192]{3,2,0,1:T(1,128)S(1)} %copy.10), channel_id=1, replica_groups=mesh['groups'=2,'vocab'=8,'mp'=2] {'mp'}, dimensions={1} | all-to-all | bytes 131072 | tf_op jit(solution)/shard_map/all_to_all | solution.py:44
  66.0 0.1 reduce_sum.38
  66.1 0.0 copy-done
  66.2 0.7 multiply_reduce_fusion
  67.5 0.1 convert_bitcast_fusion
  67.6 19.5 %all-gather.4 = bf16[16,1,8192]{2,1,0:T(2,128)(2,1)S(1)} all-gather(bf16[1,1,8192]{2,1,0:T(2,128)(2,1)S(1)} %convert_bitcast_fusion), channel_id=1, replica_groups=mesh['groups'=2,'vocab'=8,'mp'=2] {'vocab','mp'}, dimensions={0}, use_global_device_ids=true | all-gather | bytes 278528 | tf_op jit(solution)/shard_map/all_gather | solution.py:61
  87.0 0.3 constant_dynamic-slice_fusion.3
  87.3 4.0 %fusion.7 = f32[16,504]{1,0:T(8,128)} fusion(bf16[4096,504]{0,1:T(8,128)(2,1)} %param.14, bf16[16,1,4096]{2,1,0:T(2,128)(2,1)S(1)} %constant_dynamic-slice_fusion.3), kind=kOutput, calls=%fused_computation.11 | convolution fusion | flops 66060288 | bytes 4292096 | tf_op jit(solution)/shard_map/dot_general | solution.py:66
  91.3 0.0 reduce-scatter.2.cloned.1.call-update
  91.3 0.0 copy-done.2
  91.4 0.0 copy-done.3
  91.4 0.6 dynamic-slice
  92.7 4.2 %reduce-scatter.2.cloned.1.call-done = f32[8,504]{1,0:T(8,128)} async-done(((f32[16,504]{1,0:T(8,128)}), f32[8,504]{1,0:T(8,128)}) %reduce-scatter.2.cloned.1.call-update) | async-done | bytes 16144 | tf_op jit(solution)/shard_map/reduce_scatter | solution.py:67
  96.8 0.8 reduce_max.9
  97.7 0.2 dynamic-update-slice
  97.9 0.9 select_reduce_fusion
  98.9 0.2 dynamic-update-slice.2
  99.1 0.2 dynamic-update-slice.1
  99.3 21.5 %all-reduce.3 = (f32[64]{0:T(128)S(1)}, f32[64]{0:T(128)S(1)}, f32[64]{0:T(128)S(1)}) all-reduce(f32[64]{0:T(128)S(1)} %dynamic-update-slice, f32[64]{0:T(128)S(1)} %dynamic-update-slice.1, f32[64]{0:T(128)S(1)} %dynamic-update-slice.2), channel_id=2, replica_groups=mesh['groups'=2,'vocab'=8,'mp'=2] {'vocab'}, use_global_device_ids=true, to_apply=%add | all-reduce | flops 192 | bytes 1536
  120.9 0.1 reshape.20
  120.9 0.1 reshape.21
  121.0 0.1 reshape.22
  121.1 0.3 while.19
  121.4 0.5 log_subtract_fusion
  (13 shorter events, 0.3 us)
Async XLA Ops:
  6.5 84.8 %copy-start.3 = (u32[32]{0:T(128)S(1)}, u32[32]{0:T(128)}, u32[]{:S(2)}) copy-start(u32[32]{0:T(128)} %constant.71) | copy-start | bytes 388
  6.5 48.8 %copy-start.1 = (bf16[8192]{0:T(1024)(128)(2,1)S(1)}, bf16[8192]{0:T(1024)(128)(2,1)}, u32[]{:S(2)}) copy-start(bf16[8192]{0:T(1024)(128)(2,1)} %param.13) | copy-start | bytes 49156
  6.5 59.6 %copy-start = (bf16[1,8192]{1,0:T(2,128)(2,1)S(1)}, bf16[1,8192]{1,0:T(2,128)(2,1)}, u32[]{:S(2)}) copy-start(bf16[1,8192]{1,0:T(2,128)(2,1)} %param.12) | copy-start | bytes 49156
  6.5 84.8 %copy-start.2 = (s32[8]{0:T(128)S(1)}, s32[8]{0:T(128)}, u32[]{:S(2)}) copy-start(s32[8]{0:T(128)} %param.15) | copy-start | bytes 100
  49.7 12.4 %all-to-all-start = ((f32[8,2,1,1024]{3,1,2,0:T(2,128)}), f32[8,2,1,1024]{3,1,2,0:T(2,128)S(1)}, u32[]{:S(2)}, u32[]{:S(2)}) async-start(f32[8,2,1,1024]{3,1,2,0:T(2,128)} %bitcast.4), calls=%async_computation | async-start | bytes 131072 | tf_op jit(solution)/shard_map/all_to_all | solution.py:45
  55.2 41.6 %reduce-scatter.2.cloned.1.call-start = ((), (), s32[]{:S(2)}) async-start(), calls=%async_computation.3 | async-start | bytes 49152 | tf_op jit(solution)/shard_map/reduce_scatter | solution.py:67
Sparse Core Ops, SparseCore 0:
  91.4 5.3 reduce-scatter.1
where the time goes:
time: 129 us
  blocking collectives  77.3 us (60%)
  between operations  14.9 us (12%)
  matrix products  13 us (10%)
  waiting for transfers between devices  11 us (9%)
  starting transfers between devices  5.54 us (4%)
  other arithmetic  4.22 us (3%)
  local copies, waits for them, and re-layouts  2.68 us (2%)
    all_gather x1, blocking collectives, body(): lax.all_gather(gated_units, 'vocab', axis=0, tiled=True)  32.5 us
    unnamed x1, blocking collectives  21.5 us
    all_gather x1, blocking collectives, body(): lax.all_gather(normed, ('vocab', 'mp'), axis=0, tiled=True)  19.5 us
    dot_general x1, matrix products, body(): lax.dot_general(lax.all_gather(gated_units, 'vocab', axis=0, tiled=True),...  9.05 us
    all_to_all x1, waiting for transfers between devices, body(): lax.all_to_all(grouped, 'vocab', split_axis=0, concat_axis=3, tiled=True)  6.83 us
    all_to_all x1, starting transfers between devices, body(): lax.all_to_all(grouped, 'vocab', split_axis=0, concat_axis=3, tiled=True)  5.51 us
    reduce_scatter x1, waiting for transfers between devices, body(): lax.psum_scatter(logit_terms, 'mp', scatter_dimension=0, tiled=True)  4.19 us
    dot_general x1, matrix products, body(): jnp.dot(halves, head_weight, preferred_element_type=jnp.float32)  3.98 us
  transfers between devices with their start and end apart: 2, of which 2 were waited for; matrix products, arithmetic and copies ran while one was open for 1% of the time, Pallas kernels for 0%

commit v1 on v0

--- a/solution.py
+++ b/solution.py
@@ -4,6 +4,18 @@
 from jax.sharding import PartitionSpec as P
 
 EPSILON = 1e-05
+
+
+def gather_by_bits(value, axis, dim):
+    ways, here, step = (lax.axis_size(axis), lax.axis_index(axis), value.shape[dim])
+    line, have = (value, 1)
+    while have < ways:
+        line = jnp.concatenate(
+            [line, lax.ppermute(line, axis, [(d, (d - have) % ways) for d in range(ways)])],
+            axis=dim,
+        )
+        have = 2 * have
+    return jnp.roll(line, here * step, axis=dim)
 
 
 def merged_2(value, axis, combine):
@@ -33,7 +45,7 @@
         jnp.bfloat16
     )
     down_terms = lax.dot_general(
-        lax.all_gather(gated_units, "vocab", axis=0, tiled=True),
+        gather_by_bits(gated_units, "vocab", 0),
         down_weight,
         (((1,), (1,)), ((), ())),
         preferred_element_type=jnp.float32,

time: 129 us -> 118 us (0.915)
  blocking collectives: 77.3 us -> 44.8 us
  waiting for transfers between devices: 11 us -> 21.9 us
  starting transfers between devices: 5.54 us -> 15.4 us
    all_gather x1 -> x0, blocking collectives: 32.5 us -> none  [body(): lax.all_gather(gated_units, 'vocab', axis=0, tiled=True)]
    ppermute x0 -> x3, waiting for transfers between devices: none -> 10.9 us  [gather_by_bits(): lax.ppermute(line, axis, [(d, (d - have) % ways) for d in range(ways)])]
    ppermute x0 -> x3, starting transfers between devices: none -> 7.93 us  [gather_by_bits(): lax.ppermute(line, axis, [(d, (d - have) % ways) for d in range(ways)])]
    all_to_all x1, starting transfers between devices: 5.51 us -> 7.47 us  [body(): lax.all_to_all(grouped, 'vocab', split_axis=0, concat_axis=3, tiled=True)]
  transfers between devices with their start and end apart: 2 -> 5, of which waited for: 2 -> 5; matrix products, arithmetic and copies ran while one was open for 1% -> 1% of each run, Pallas kernels for 0% -> 0%
where the time goes in v1:
time: 118 us; the launch traced here: 117 us
  blocking collectives  44.8 us (38%)
  waiting for transfers between devices  21.9 us (19%)
  starting transfers between devices  15.4 us (13%)
  between operations  14.9 us (13%)
  matrix products  13 us (11%)
  other arithmetic  4.39 us (4%)
  local copies, waits for them, and re-layouts  2.85 us (2%)
    unnamed x1, blocking collectives  21.5 us
    all_gather x1, blocking collectives, body(): lax.all_gather(normed, ('vocab', 'mp'), axis=0, tiled=True)  19.5 us
    ppermute x3, waiting for transfers between devices, gather_by_bits(): lax.ppermute(line, axis, [(d, (d - have) % ways) for d in range(ways)])  10.9 us
    dot_general x1, matrix products, body(): lax.dot_general(gather_by_bits(gated_units, 'vocab', 0), down_weight, (((...  9.06 us
    ppermute x3, starting transfers between devices, gather_by_bits(): lax.ppermute(line, axis, [(d, (d - have) % ways) for d in range(ways)])  7.93 us
    all_to_all x1, starting transfers between devices, body(): lax.all_to_all(grouped, 'vocab', split_axis=0, concat_axis=3, tiled=True)  7.47 us
    all_to_all x1, waiting for transfers between devices, body(): lax.all_to_all(grouped, 'vocab', split_axis=0, concat_axis=3, tiled=True)  6.83 us
    reduce_scatter x1, waiting for transfers between devices, body(): lax.psum_scatter(logit_terms, 'mp', scatter_dimension=0, tiled=True)  4.19 us
  transfers between devices with their start and end apart: 5, of which 5 were waited for; matrix products, arithmetic and copies ran while one was open for 1% of the time, Pallas kernels for 0%

profile of v1, /device:TPU:0, one launch (start us, length us, event | category | flops | bytes accessed | tf_op | source)
XLA Modules:
  0.0 117.4 jit_solution(11887827784243195205)
XLA Ops:
  6.5 0.0 copy-start.3
  6.5 0.0 copy-start.1
  6.5 0.0 copy-start
  6.5 0.0 copy-start.2
  6.5 0.9 fusion.13
  7.4 6.1 %collective-permute-start = (bf16[2,7168]{1,0:T(2,128)(2,1)S(1)}, bf16[2,7168]{1,0:T(2,128)(2,1)S(1)}, u32[]{:S(2)}, u32[]{:S(2)}) collective-permute-start(bf16[2,7168]{1,0:T(2,128)(2,1)S(1)} %fusion.13), channel_id=1, source_target_pairs={{0,14},{2,0},{4,2},{6,4},{8,6},{10,8},{12,10},{14,12},{1,15},{3,1}... | collective-permute-start | bytes 86024 | tf_op jit(solution)/shard_map/ppermute | solution.py:14
  13.5 1.6 %collective-permute-done = bf16[2,7168]{1,0:T(2,128)(2,1)S(1)} collective-permute-done((bf16[2,7168]{1,0:T(2,128)(2,1)S(1)}, bf16[2,7168]{1,0:T(2,128)(2,1)S(1)}, u32[]{:S(2)}, u32[]{:S(2)}) %collective-permute-start) | collective-permute-done | bytes 28704 | tf_op jit(solution)/shard_map/ppermute | solution.py:14
  15.0 0.1 pad_maximum_fusion.1
  15.1 1.4 %collective-permute-start.1 = (bf16[4,7168]{1,0:T(4,128)(2,1)S(1)}, bf16[4,7168]{1,0:T(4,128)(2,1)S(1)}, u32[]{:S(2)}, u32[]{:S(2)}) collective-permute-start(bf16[4,7168]{1,0:T(4,128)(2,1)S(1)} %pad_maximum_fusion.1), channel_id=1, source_target_pairs={{0,12},{2,14},{4,0},{6,2},{8,4},{10,6},{12,8},{14,10},{1,13},{3,15... | collective-permute-start | bytes 172040 | tf_op jit(solution)/shard_map/ppermute | solution.py:14
  16.5 2.8 %collective-permute-done.1 = bf16[4,7168]{1,0:T(4,128)(2,1)S(1)} collective-permute-done((bf16[4,7168]{1,0:T(4,128)(2,1)S(1)}, bf16[4,7168]{1,0:T(4,128)(2,1)S(1)}, u32[]{:S(2)}, u32[]{:S(2)}) %collective-permute-start.1) | collective-permute-done | bytes 57376 | tf_op jit(solution)/shard_map/ppermute | solution.py:14
  19.3 0.1 pad_maximum_fusion
  19.4 0.4 collective-permute-start.2
  19.9 6.5 %collective-permute-done.2 = bf16[8,7168]{1,0:T(8,128)(2,1)S(1)} collective-permute-done((bf16[8,7168]{1,0:T(8,128)(2,1)S(1)}, bf16[8,7168]{1,0:T(8,128)(2,1)S(1)}, u32[]{:S(2)}, u32[]{:S(2)}) %collective-permute-start.2) | collective-permute-done | bytes 114720 | tf_op jit(solution)/shard_map/ppermute | solution.py:14
  26.4 0.3 concatenate.16
  26.7 9.1 %fusion.7 = f32[16,1024]{1,0:T(8,128)S(1)} fusion(bf16[1024,7168]{1,0:T(8,128)(2,1)} %param.11, bf16[32,7168]{1,0:T(8,128)(2,1)S(1)} %concatenate.16, s32[]{:T(128)S(6)} %select_n.33), kind=kOutput, calls=%fused_computation.10 | convolution fusion | flops 234881024 | bytes 14974980 | tf_op jit(solution)/shard_map/dot_general | solution.py:47
  35.7 0.7 reshape.18
  36.4 7.5 %all-to-all-start = ((f32[8,2,1,1024]{3,1,2,0:T(2,128)}), f32[8,2,1,1024]{3,1,2,0:T(2,128)S(1)}, u32[]{:S(2)}, u32[]{:S(2)}) async-start(f32[8,2,1,1024]{3,1,2,0:T(2,128)} %bitcast.3), calls=%async_computation | async-start | bytes 131072 | tf_op jit(solution)/shard_map/all_to_all | solution.py:57
  43.9 0.0 reduce-scatter.2.cloned.1.call-start
  43.9 0.0 copy-done.1
  44.0 6.8 %all-to-all-done = f32[8,2,1,1024]{3,1,2,0:T(2,128)S(1)} async-done(((f32[8,2,1,1024]{3,1,2,0:T(2,128)}), f32[8,2,1,1024]{3,1,2,0:T(2,128)S(1)}, u32[]{:S(2)}, u32[]{:S(2)}) %all-to-all-start) | async-done | bytes 65568 | tf_op jit(solution)/shard_map/all_to_all | solution.py:57
  50.8 0.1 copy.10
  50.9 3.8 %all_to_all.27 = f32[1,2,1,8192]{3,2,0,1:T(1,128)S(1)} all-to-all(f32[1,2,1,8192]{3,2,0,1:T(1,128)S(1)} %copy.10), channel_id=1, replica_groups=mesh['groups'=2,'vocab'=8,'mp'=2] {'mp'}, dimensions={1} | all-to-all | bytes 131072 | tf_op jit(solution)/shard_map/all_to_all | solution.py:56
  54.7 0.1 reduce_sum.38
  54.7 0.0 copy-done
  54.8 0.7 multiply_reduce_fusion
  56.2 0.1 convert_bitcast_fusion
  56.2 19.5 %all-gather.3 = bf16[16,1,8192]{2,1,0:T(2,128)(2,1)S(1)} all-gather(bf16[1,1,8192]{2,1,0:T(2,128)(2,1)S(1)} %convert_bitcast_fusion), channel_id=1, replica_groups=mesh['groups'=2,'vocab'=8,'mp'=2] {'vocab','mp'}, dimensions={0}, use_global_device_ids=true | all-gather | bytes 278528 | tf_op jit(solution)/shard_map/all_gather | solution.py:73
  75.7 0.3 constant_dynamic-slice_fusion.3
  76.0 4.0 %fusion.9 = f32[16,504]{1,0:T(8,128)} fusion(bf16[4096,504]{0,1:T(8,128)(2,1)} %param.14, bf16[16,1,4096]{2,1,0:T(2,128)(2,1)S(1)} %constant_dynamic-slice_fusion.3), kind=kOutput, calls=%fused_computation.13 | convolution fusion | flops 66060288 | bytes 4292096 | tf_op jit(solution)/shard_map/dot_general | solution.py:78
  79.9 0.0 reduce-scatter.2.cloned.1.call-update
  80.0 0.0 copy-done.2
  80.0 0.0 copy-done.3
  80.0 0.6 dynamic-slice
  81.3 4.2 %reduce-scatter.2.cloned.1.call-done = f32[8,504]{1,0:T(8,128)} async-done(((f32[16,504]{1,0:T(8,128)}), f32[8,504]{1,0:T(8,128)}) %reduce-scatter.2.cloned.1.call-update) | async-done | bytes 16144 | tf_op jit(solution)/shard_map/reduce_scatter | solution.py:79
  85.5 0.8 reduce_max.9
  86.3 0.2 dynamic-update-slice
  86.6 0.9 select_reduce_fusion
  87.5 0.2 dynamic-update-slice.2
  87.7 0.2 dynamic-update-slice.1
  88.0 21.5 %all-reduce.3 = (f32[64]{0:T(128)S(1)}, f32[64]{0:T(128)S(1)}, f32[64]{0:T(128)S(1)}) all-reduce(f32[64]{0:T(128)S(1)} %dynamic-update-slice, f32[64]{0:T(128)S(1)} %dynamic-update-slice.1, f32[64]{0:T(128)S(1)} %dynamic-update-slice.2), channel_id=2, replica_groups=mesh['groups'=2,'vocab'=8,'mp'=2] {'vocab'}, use_global_device_ids=true, to_apply=%add | all-reduce | flops 192 | bytes 1536
  109.5 0.1 reshape.20
  109.6 0.1 reshape.21
  109.6 0.1 reshape.22
  109.7 0.3 while.19
  110.0 0.5 log_subtract_fusion
  (13 shorter events, 0.3 us)
Async XLA Ops:
  6.5 73.5 %copy-start.3 = (u32[32]{0:T(128)S(1)}, u32[32]{0:T(128)}, u32[]{:S(2)}) copy-start(u32[32]{0:T(128)} %constant.94) | copy-start | bytes 388
  6.5 37.4 %copy-start.1 = (bf16[8192]{0:T(1024)(128)(2,1)S(1)}, bf16[8192]{0:T(1024)(128)(2,1)}, u32[]{:S(2)}) copy-start(bf16[8192]{0:T(1024)(128)(2,1)} %param.13) | copy-start | bytes 49156
  6.5 48.2 %copy-start = (bf16[1,8192]{1,0:T(2,128)(2,1)S(1)}, bf16[1,8192]{1,0:T(2,128)(2,1)}, u32[]{:S(2)}) copy-start(bf16[1,8192]{1,0:T(2,128)(2,1)} %param.12) | copy-start | bytes 49156
  6.5 73.4 %copy-start.2 = (s32[8]{0:T(128)S(1)}, s32[8]{0:T(128)}, u32[]{:S(2)}) copy-start(s32[8]{0:T(128)} %param.15) | copy-start | bytes 100
  7.4 7.6 %collective-permute-start = (bf16[2,7168]{1,0:T(2,128)(2,1)S(1)}, bf16[2,7168]{1,0:T(2,128)(2,1)S(1)}, u32[]{:S(2)}, u32[]{:S(2)}) collective-permute-start(bf16[2,7168]{1,0:T(2,128)(2,1)S(1)} %fusion.13), channel_id=1, source_target_pairs={{0,14},{2,0},{4,2},{6,4},{8,6},{10,8},{12,10},{14,12},{1,15},{3,1}... | collective-permute-start | bytes 86024 | tf_op jit(solution)/shard_map/ppermute | solution.py:14
  15.1 4.2 %collective-permute-start.1 = (bf16[4,7168]{1,0:T(4,128)(2,1)S(1)}, bf16[4,7168]{1,0:T(4,128)(2,1)S(1)}, u32[]{:S(2)}, u32[]{:S(2)}) collective-permute-start(bf16[4,7168]{1,0:T(4,128)(2,1)S(1)} %pad_maximum_fusion.1), channel_id=1, source_target_pairs={{0,12},{2,14},{4,0},{6,2},{8,4},{10,6},{12,8},{14,10},{1,13},{3,15... | collective-permute-start | bytes 172040 | tf_op jit(solution)/shard_map/ppermute | solution.py:14
  19.4 7.0 %collective-permute-start.2 = (bf16[8,7168]{1,0:T(8,128)(2,1)S(1)}, bf16[8,7168]{1,0:T(8,128)(2,1)S(1)}, u32[]{:S(2)}, u32[]{:S(2)}) collective-permute-start(bf16[8,7168]{1,0:T(8,128)(2,1)S(1)} %pad_maximum_fusion), channel_id=1, source_target_pairs={{0,8},{2,10},{4,12},{6,14},{8,0},{10,2},{12,4},{14,6},{1,9},{3,11}... | collective-permute-start | bytes 344072 | tf_op jit(solution)/shard_map/ppermute | solution.py:14
  36.4 14.4 %all-to-all-start = ((f32[8,2,1,1024]{3,1,2,0:T(2,128)}), f32[8,2,1,1024]{3,1,2,0:T(2,128)S(1)}, u32[]{:S(2)}, u32[]{:S(2)}) async-start(f32[8,2,1,1024]{3,1,2,0:T(2,128)} %bitcast.3), calls=%async_computation | async-start | bytes 131072 | tf_op jit(solution)/shard_map/all_to_all | solution.py:57
  43.9 41.6 %reduce-scatter.2.cloned.1.call-start = ((), (), s32[]{:S(2)}) async-start(), calls=%async_computation.3 | async-start | bytes 49152 | tf_op jit(solution)/shard_map/reduce_scatter | solution.py:79
Sparse Core Ops, SparseCore 0:
  80.1 5.3 reduce-scatter.1
